TPU v7x, 512 devices: a whole 4x8x8 slice. The times are simulated.
512 devices in a mesh: row: 16 (over x_lo, y), col: 32 (over x_hi, z, core).
Axes of the slice: x: 4 (x_hi: 2, x_lo: 2; x = x_hi * 2 + x_lo), y: 8, z: 8, core: 2. Of those that a mesh axis runs over, the one named last changes fastest.
Arguments:
- tokens: bfloat16 [2048, 6144], P('row', 'col'), may hold values from -6 to 6
- w_query: bfloat16 [6144, 4096], P('row', 'col'), may hold values from -0.078125 to 0.078125
- w_key: bfloat16 [6144, 4096], P('row', 'col'), may hold values from -0.078125 to 0.078125
- w_value: bfloat16 [6144, 4096], P('row', 'col'), may hold values from -0.078125 to 0.078125
- w_out: bfloat16 [4096, 6144], P('row', 'col'), may hold values from -0.09375 to 0.09375
- key_cache: bfloat16 [32768, 4096], P('row', 'col'), may hold values from -6 to 6
- value_cache: bfloat16 [32768, 4096], P('row', 'col'), may hold values from -6 to 6
- query_gain: float32 [128], replicated, may hold values from 1 to 2.5
- key_gain: float32 [128], replicated, may hold values from 1 to 2.5
- out_gate: float32 [6144], P('col'), may hold values from 0.5 to 2
- cotangent: bfloat16 [2048, 6144], P('row', 'col'), may hold values from -6 to 6
Outputs:
- layer_out: bfloat16 [2048, 6144], P('row', 'col')
- attention_cotangent: bfloat16 [2048, 4096], P('row', 'col')
All inputs are finite; a program needn't handle non-finite values.
Results may differ from a plain program's by a relative error of at most 0.012.
Values may be sent and summed in bfloat16 or wider, within the bound.
A program may use at most 64 MiB of HBM per device.

v0:
```python
import jax
import jax.numpy as jnp
from jax import lax
from jax.sharding import PartitionSpec as P

epsilon = 1e-06


def norm_heads(values, gain):
    wide = values.astype(jnp.float32)
    mean_square = jnp.mean(wide * wide, axis=-1, keepdims=True)
    return (wide * lax.rsqrt(mean_square + epsilon) * gain).astype(jnp.bfloat16)


def body(
    tokens,
    w_query,
    w_key,
    w_value,
    w_out,
    key_cache,
    value_cache,
    query_gain,
    key_gain,
    out_gate,
    cotangent,
):
    tok_rows = tokens.shape[0]
    head_size = query_gain.shape[0]
    local_width = w_query.shape[1]
    heads_here = local_width // head_size
    scale = head_size ** (-0.5)
    features_whole = lax.all_gather(tokens, "col", axis=1, tiled=True)
    pieces = (
        lax.all_gather(w_query, "row", axis=0, tiled=True),
        lax.all_gather(w_key, "row", axis=0, tiled=True),
        lax.all_gather(w_value, "row", axis=0, tiled=True),
    )
    proj_query, proj_key, proj_value = tuple(
        (jnp.dot(features_whole, piece, preferred_element_type=jnp.float32) for piece in pieces)
    )
    query_norm = norm_heads(
        proj_query.astype(jnp.bfloat16).reshape(tok_rows, heads_here, head_size), query_gain
    ).reshape(tok_rows, local_width)
    keys_local = jnp.concatenate([key_cache, proj_key.astype(jnp.bfloat16)], axis=0)
    key_norm = norm_heads(keys_local.reshape(-1, heads_here, head_size), key_gain)
    values_local = jnp.concatenate([value_cache, proj_value.astype(jnp.bfloat16)], axis=0).reshape(
        -1, heads_here, head_size
    )
    queries = lax.all_gather(query_norm, "row", axis=0, tiled=True)
    total_rows = queries.shape[0]
    block_rows = min(512, total_rows)
    query_blocks = queries.reshape(total_rows // block_rows, block_rows, heads_here, head_size)

    def attend(query_block):
        scores = (
            jnp.einsum("qhd,khd->hqk", query_block, key_norm, preferred_element_type=jnp.float32)
            * scale
        )
        weights = jnp.exp(scores)
        sums_here = jnp.sum(weights, axis=2)
        numerators = jnp.einsum(
            "hqk,khd->qhd",
            weights.astype(jnp.bfloat16),
            values_local,
            preferred_element_type=jnp.float32,
        )
        return (numerators, sums_here.T)

    numerators, sums_local = lax.map(attend, query_blocks)
    numerators = numerators.reshape(total_rows, local_width)
    sums_local = sums_local.reshape(total_rows, heads_here)
    numer_mine, sums_mine = (
        lax.psum_scatter(numerators, "row", scatter_dimension=0, tiled=True),
        lax.psum_scatter(sums_local, "row", scatter_dimension=0, tiled=True),
    )
    attention = (
        (numer_mine.reshape(tok_rows, heads_here, head_size) / sums_mine[:, :, None])
        .astype(jnp.bfloat16)
        .reshape(tok_rows, local_width)
    )
    attention_whole = lax.all_gather(attention, "col", axis=1, tiled=True)
    scaled = (cotangent.astype(jnp.float32) * out_gate).astype(jnp.bfloat16)
    contract_last = (((1,), (1,)), ((), ()))
    output_whole = lax.all_gather(w_out, "row", axis=0, tiled=True)
    branch = jnp.dot(attention_whole, output_whole, preferred_element_type=jnp.float32)
    grad_terms = lax.dot_general(
        scaled, output_whole, contract_last, preferred_element_type=jnp.float32
    )
    attention_cotangent = lax.psum_scatter(
        grad_terms, "col", scatter_dimension=1, tiled=True
    ).astype(jnp.bfloat16)
    layer_out = (tokens.astype(jnp.float32) + out_gate * branch).astype(jnp.bfloat16)
    return (layer_out, attention_cotangent)


def solution(mesh):
    placed = (
        P("row", "col"),
        P("row", "col"),
        P("row", "col"),
        P("row", "col"),
        P("row", "col"),
        P("row", "col"),
        P("row", "col"),
        P(),
        P(),
        P("col"),
        P("row", "col"),
    )
    return jax.shard_map(
        body,
        mesh=mesh,
        in_specs=placed,
        out_specs=(P("row", "col"), P("row", "col")),
        check_vma=False,
    )
```

profile of v0, /device:TPU:1, one launch (start us, length us, event | category | flops | bytes accessed | tf_op | source)
XLA Modules:
  0.0 756.0 jit_solution(9528778600435465140)
XLA Ops:
  7.2 0.0 all-gather.11.cloned.1.call-start
  7.2 0.7 all-gather.11.cloned.1.call-update
  7.9 0.0 all-gather.7.cloned.1.call-start
  7.9 0.7 all-gather.7.cloned.1.call-update
  8.6 0.0 all-gather.9.cloned.1.call-start
  8.7 0.7 all-gather.9.cloned.1.call-update
  9.4 0.0 all-gather.13.cloned.1.call-start
  9.4 0.5 all-gather.13.cloned.1.call-update
  10.0 0.0 all-gather.17.cloned.1.call-start
  10.0 0.5 all-gather.17.cloned.1.call-update
  10.5 0.0 reduce-scatter.10.cloned.1.call-start
  10.6 0.0 copy-start.2
  10.6 67.1 %all-gather.11.cloned.1.call-done = bf16[6144,128]{1,0:T(8,128)(2,1)} async-done(((bf16[384,128]{1,0:T(8,128)(2,1)}), bf16[6144,128]{1,0:T(8,128)(2,1)}) %all-gather.11.cloned.1.call-update) | async-done | bytes 1572880 | tf_op jit(solution)/shard_map/all_gather | solution.py:36
  77.7 96.2 %all-gather.7.cloned.1.call-done = bf16[128,6144]{0,1:T(8,128)(2,1)} async-done(((bf16[128,192]{0,1:T(8,128)(2,1)}), bf16[128,6144]{0,1:T(8,128)(2,1)}) %all-gather.7.cloned.1.call-update) | async-done | bytes 1572880 | tf_op jit(solution)/shard_map/all_gather | solution.py:33
  173.9 2.6 fusion.20
  176.5 0.0 copy-done.2
  176.5 0.4 fusion.17
  176.9 0.0 copy-start.9
  177.0 57.0 %all-gather.9.cloned.1.call-done = bf16[6144,128]{1,0:T(8,128)(2,1)} async-done(((bf16[384,128]{1,0:T(8,128)(2,1)}), bf16[6144,128]{1,0:T(8,128)(2,1)}) %all-gather.9.cloned.1.call-update) | async-done | bytes 1572880 | tf_op jit(solution)/shard_map/all_gather | solution.py:35
  234.0 0.0 copy-done
  234.0 2.0 multiply_reduce_fusion
  236.1 0.0 copy-done.9
  236.1 1.2 fusion.19
  237.2 68.7 %all-gather.13.cloned.1.call-done = bf16[6144,128]{1,0:T(8,128)(2,1)} async-done(((bf16[384,128]{1,0:T(8,128)(2,1)}), bf16[6144,128]{1,0:T(8,128)(2,1)}) %all-gather.13.cloned.1.call-update) | async-done | bytes 1572880 | tf_op jit(solution)/shard_map/all_gather | solution.py:37
  305.9 2.1 convolution_convert_fusion
  308.0 0.0 copy-done.5
  308.0 0.0 copy-start.4
  308.1 0.0 copy-done.10
  308.1 0.1 multiply_convert_fusion.1
  308.2 27.3 %all_gather.23 = bf16[2048,128]{0,1:T(8,128)(2,1)S(1)} all-gather(bf16[128,128]{0,1:T(8,128)(2,1)S(1)} %multiply_convert_fusion.1), channel_id=1, replica_groups=mesh['row'=16,'col'=32] {'row'}, dimensions={0}, use_global_device_ids=true | all-gather | bytes 557056 | tf_op jit(solution)/shard_map/all_gather | solution.py:50
  335.4 1.0 copy.17
  336.5 0.0 copy-done.4
  336.5 10.8 %while.12 = (s32[]{:T(128)}, f32[4,512,1,128]{3,1,2,0:T(8,128)S(1)}, f32[4,512,1]{1,2,0:T(1,128)S(1)}, bf16[4,512,1,128]{3,1,2,0:T(8,128)(2,1)}, bf16[2176,1,128...) while((s32[]{:T(128)}, f32[4,512,1,128]{3,1,2,0:T(8,128)S(1)}, ...), condition=%wide.region_4.5_spmd, body=%wide.region_2.4_spmd.sunk | while | flops 573767168 | bytes 5970517 | solution.py:70
  336.5 1.9 fusion.40
  338.4 0.8 fusion.41
  339.2 1.9 fusion.40
  341.1 0.8 fusion.41
  341.9 1.9 fusion.40
  343.8 0.8 fusion.41
  344.6 1.9 fusion.40
  346.5 0.8 fusion.41
  347.3 0.0 copy-start.3
  347.3 0.0 copy-start.7
  347.3 0.0 copy-start.8
  347.3 1.4 copy.18
  348.7 0.0 reduce-scatter.10.cloned.1.call-update
  348.7 0.0 reduce-scatter.6.cloned.1.call-start
  348.8 0.7 reduce-scatter.6.cloned.1.call-update
  349.5 0.0 reduce-scatter.8.cloned.1.call-start
  349.5 26.5 %all-gather.17.cloned.1.call-done = bf16[4096,192]{0,1:T(8,128)(2,1)} async-done(((bf16[256,192]{0,1:T(8,128)(2,1)}), bf16[4096,192]{0,1:T(8,128)(2,1)}) %all-gather.17.cloned.1.call-update) | async-done | bytes 1572880 | tf_op jit(solution)/shard_map/all_gather | solution.py:85
  376.1 0.0 copy-done.8
  376.1 3.3 fusion.21
  379.4 0.0 reduce-scatter.8.cloned.1.call-update
  379.4 0.0 all-gather.15.cloned.1.call-start
  379.5 72.9 %reduce-scatter.10.cloned.1.call-done = f32[128,1]{1,0:T(8,128)} async-done(((f32[2048,1]{1,0:T(8,128)}), f32[128,1]{1,0:T(8,128)}) %reduce-scatter.10.cloned.1.call-update) | async-done | bytes 528
  452.4 0.9 copy.19
  453.3 73.1 %reduce-scatter.6.cloned.1.call-done = f32[128,128]{1,0:T(8,128)} async-done(((f32[2048,128]{1,0:T(8,128)}), f32[128,128]{1,0:T(8,128)}) %reduce-scatter.6.cloned.1.call-update) | async-done | bytes 65552 | tf_op jit(solution)/shard_map/reduce_scatter | solution.py:74
  526.4 1.5 divide_convert_fusion
  528.0 0.0 all-gather.15.cloned.1.call-update
  528.0 134.1 %reduce-scatter.8.cloned.1.call-done = f32[128,128]{1,0:T(8,128)} async-done(((f32[128,4096]{1,0:T(8,128)}), f32[128,128]{1,0:T(8,128)}) %reduce-scatter.8.cloned.1.call-update) | async-done | bytes 65552 | tf_op jit(solution)/shard_map/reduce_scatter | solution.py:90
  662.0 1.5 convert_element_type.78
  663.5 83.6 %all-gather.15.cloned.1.call-done = bf16[128,4096]{1,0:T(8,128)(2,1)} async-done(((bf16[128,128]{1,0:T(8,128)(2,1)}), bf16[128,4096]{1,0:T(8,128)(2,1)}) %all-gather.15.cloned.1.call-update) | async-done | bytes 1048592 | tf_op jit(solution)/shard_map/all_gather | solution.py:82
  747.1 0.0 copy-done.1
  747.1 2.4 fusion.15
  (17 shorter events, 0.1 us)
Async XLA Ops:
  7.2 70.5 %all-gather.11.cloned.1.call-start = ((), (), s32[]{:S(2)}) async-start(), calls=%async_computation.5 | async-start | bytes 1671168 | tf_op jit(solution)/shard_map/all_gather | solution.py:36
  7.9 166.0 %all-gather.7.cloned.1.call-start = ((), (), s32[]{:S(2)}) async-start(), calls=%async_computation.3 | async-start | bytes 1622016 | tf_op jit(solution)/shard_map/all_gather | solution.py:33
  8.6 225.4 %all-gather.9.cloned.1.call-start = ((), (), s32[]{:S(2)}) async-start(), calls=%async_computation.4 | async-start | bytes 1671168 | tf_op jit(solution)/shard_map/all_gather | solution.py:35
  9.4 296.5 %all-gather.13.cloned.1.call-start = ((), (), s32[]{:S(2)}) async-start(), calls=%async_computation.6 | async-start | bytes 1671168 | tf_op jit(solution)/shard_map/all_gather | solution.py:37
  10.0 366.1 %all-gather.17.cloned.1.call-start = ((), (), s32[]{:S(2)}) async-start(), calls=%async_computation.9 | async-start | bytes 1671168 | tf_op jit(solution)/shard_map/all_gather | solution.py:85
  10.5 441.8 %reduce-scatter.10.cloned.1.call-start = ((), (), s32[]{:S(2)}) async-start(), calls=%async_computation.11 | async-start | bytes 1114112
  10.6 165.9 %copy-start.2 = (bf16[2048,128]{1,0:T(8,128)(2,1)S(1)}, bf16[2048,128]{1,0:T(8,128)(2,1)}, u32[]{:S(2)}) copy-start(bf16[2048,128]{1,0:T(8,128)(2,1)} %param.18) | copy-start | bytes 1572868
  173.9 60.1 %copy-start = (bf16[128,6144]{0,1:T(8,128)(2,1)S(1)}, bf16[128,6144]{0,1:T(8,128)(2,1)}, u32[]{:S(2)}) copy-start(bf16[128,6144]{0,1:T(8,128)(2,1)} %all-gather.7.cloned.1.call-done) | copy-start | bytes 4718596
  176.9 59.1 %copy-start.9 = (f32[128]{0:T(128)S(1)}, f32[128]{0:T(128)}, u32[]{:S(2)}) copy-start(f32[128]{0:T(128)} %param.21) | copy-start | bytes 1540
  237.2 70.8 %copy-start.10 = (f32[128]{0:T(128)S(1)}, f32[128]{0:T(128)}, u32[]{:S(2)}) copy-start(f32[128]{0:T(128)} %param.20) | copy-start | bytes 1540
  305.9 2.1 copy-start.5
  308.0 28.5 %copy-start.4 = (bf16[2176,1,128]{2,0,1:T(8,128)(2,1)S(1)}, bf16[2176,1,128]{2,0,1:T(8,128)(2,1)}, u32[]{:S(2)}) copy-start(bf16[2176,1,128]{2,0,1:T(8,128)(2,1)} %fusion.19) | copy-start | bytes 1671172
  347.3 1.5 copy-start.3
  347.3 28.8 %copy-start.7 = (bf16[128,192]{0,1:T(8,128)(2,1)S(1)}, bf16[128,192]{0,1:T(8,128)(2,1)}, u32[]{:S(2)}) copy-start(bf16[128,192]{0,1:T(8,128)(2,1)} %param.23) | copy-start | bytes 147460
  347.3 28.8 %copy-start.8 = (f32[192]{0:T(256)S(1)}, f32[192]{0:T(256)}, u32[]{:S(2)}) copy-start(f32[192]{0:T(256)} %param.22) | copy-start | bytes 2308
  348.7 177.7 %reduce-scatter.6.cloned.1.call-start = ((), (), s32[]{:S(2)}) async-start(), calls=%async_computation.7 | async-start | bytes 1114112 | tf_op jit(solution)/shard_map/reduce_scatter | solution.py:74
  349.5 312.5 %reduce-scatter.8.cloned.1.call-start = ((), (), s32[]{:S(2)}) async-start(), calls=%async_computation.10 | async-start | bytes 2162688 | tf_op jit(solution)/shard_map/reduce_scatter | solution.py:90
  379.4 367.7 %copy-start.1 = (bf16[4096,192]{0,1:T(8,128)(2,1)S(1)}, bf16[4096,192]{0,1:T(8,128)(2,1)}, u32[]{:S(2)}) copy-start(bf16[4096,192]{0,1:T(8,128)(2,1)} %all-gather.17.cloned.1.call-done) | copy-start | bytes 4718596
  379.4 367.7 %copy-start.6 = (bf16[128,192]{0,1:T(8,128)(2,1)S(1)}, bf16[128,192]{0,1:T(8,128)(2,1)}, u32[]{:S(2)}) copy-start(bf16[128,192]{0,1:T(8,128)(2,1)} %param.13) | copy-start | bytes 147460
  379.4 367.7 %all-gather.15.cloned.1.call-start = ((), (), s32[]{:S(2)}) async-start(), calls=%async_computation.8 | async-start | bytes 1081344 | tf_op jit(solution)/shard_map/all_gather | solution.py:82
Sparse Core Ops, SparseCore 0:
  10.0 67.5 all-gather.10
  81.0 92.8 all-gather.6
  176.0 57.9 all-gather.8
  235.9 69.9 all-gather.12
  307.8 68.2 all-gather.16
  378.7 73.6 reduce-scatter.9
  455.2 71.1 reduce-scatter.5
  531.1 130.8 reduce-scatter.7
  665.8 81.2 all-gather.14
where the time goes:
time: 756 us
  waiting for transfers between devices  683 us (90%)
  blocking collectives  27.3 us (4%)
  matrix products  23.2 us (3%)
  between operations  14 us (2%)
    reduce_scatter x1, waiting for transfers between devices, body(): lax.psum_scatter(grad_terms, 'col', scatter_dimension=1, tiled=True)  134 us
    all_gather x1, waiting for transfers between devices, body(): features_whole = lax.all_gather(tokens, 'col', axis=1, tiled=True)  96.2 us
    all_gather x1, waiting for transfers between devices, body(): attention_whole = lax.all_gather(attention, 'col', axis=1, tiled=True)  83.6 us
    unnamed x10, waiting for transfers between devices  76.7 us
    reduce_scatter x1, waiting for transfers between devices, body(): lax.psum_scatter(numerators, 'row', scatter_dimension=0, tiled=True)  73.1 us
    all_gather x1, waiting for transfers between devices, body(): lax.all_gather(w_value, 'row', axis=0, tiled=True)  68.7 us
    all_gather x1, waiting for transfers between devices, body(): lax.all_gather(w_key, 'row', axis=0, tiled=True)  67.1 us
    all_gather x1, waiting for transfers between devices, body(): lax.all_gather(w_query, 'row', axis=0, tiled=True)  57 us
  transfers between devices with their start and end apart: 9, of which 9 were waited for; matrix products, arithmetic and copies ran while one was open for 4% of the time, Pallas kernels for 0%

commit v1 on v0

v1 whole, which is shorter than its diff:
```python
import functools
import math

import jax
import jax.numpy as jnp
from jax import lax
from jax.experimental import pallas as pl
from jax.experimental.pallas import tpu as pltpu
from jax.sharding import PartitionSpec as P

MESH = pl.DeviceIdType.MESH
epsilon = 1e-06
f32 = jnp.float32
bf16 = jnp.bfloat16
LAST = (((1,), (1,)), ((), ()))


def norm_rows(values, gain):
    wide = values.astype(f32)
    mean_square = jnp.mean(wide * wide, axis=-1, keepdims=True)
    return (wide * lax.rsqrt(mean_square + epsilon) * gain).astype(bf16)


def ring_order(n):
    order = [0]
    for d in range(1, n // 2 + 1):
        order.append(d)
        if (n - d) % n != d:
            order.append(n - d)
    return order


def kernel(
    n,
    tokens,
    w_query,
    w_key,
    w_value,
    w_out,
    key_cache,
    value_cache,
    query_gain,
    key_gain,
    out_gate,
    cotangent,
    layer_out,
    grad_out,
    tok,
    wall,
    wout,
    keys,
    vals,
    scaled,
    qsend,
    qpart,
    kvsend,
    kvpart,
    queries,
    acc,
    nsend,
    nrecv,
    gsend,
    grecv,
    att,
    s_t,
    r_t,
    s_w,
    r_w,
    s_wo,
    r_wo,
    s_wx,
    r_wx,
    s_g,
    r_g,
    s_q,
    r_q,
    s_kv,
    r_kv,
    s_qa,
    r_qa,
    s_n,
    r_n,
    s_gr,
    r_gr,
    s_a,
    r_a,
):
    rows, dcols = tokens.shape
    head = query_gain.shape[1]
    cached = key_cache.shape[0]
    row = lax.axis_index("row")
    col = lax.axis_index("col")
    xl, y = row // n, row % n
    xh, z, k = col // (2 * n), (col // 2) % n, col % 2

    def dev(xl_, y_, xh_, z_, k_):
        return (xl_ * n + y_, (xh_ * n + z_) * 2 + k_)

    order = ring_order(n)
    slot_of = {d: i for i, d in enumerate(order)}

    def dist(d):
        return min(d, n - d)

    row_rel = sorted([(a, b) for b in order for a in (0, 1)], key=lambda t: dist(t[1]) + t[0])
    row_inv = [row_rel.index((a, (n - b) % n)) for a, b in row_rel]
    col_rel = [
        (a, b, c)
        for b in order
        for a in (0, 1)
        for c in (0, 1)
        if (a, b, c) != (0, 0, 0)
    ]
    col_inv = [col_rel.index((a, (n - b) % n, c)) for a, b, c in col_rel]

    def row_peer(a, b):
        return dev((xl + a) % 2, (y + b) % n, xh, z, k)

    def col_peer(a, b, c):
        return dev(xl, y, (xh + a) % 2, (z + b) % n, (k + c) % 2)

    def remote(src, dst, ssem, rsem, to):
        return pltpu.make_async_remote_copy(
            src_ref=src, dst_ref=dst, send_sem=ssem, recv_sem=rsem, device_id=to, device_id_type=MESH
        )

    any_peer = col_peer(0, 0, 1)

    def arrived(dst, ssem, rsem):
        remote(dst, dst, ssem, rsem, any_peer).wait_recv()

    sends = []

    def send(src, dst, ssem, rsem, to):
        copy = remote(src, dst, ssem, rsem, to)
        copy.start()
        sends.append(copy)

    barrier = pltpu.get_barrier_semaphore()
    off_diagonal = y != z
    twin = dev(xl, z, xh, y, k)

    @pl.when(off_diagonal)
    def _():
        pl.semaphore_signal(barrier, inc=1, device_id=twin, device_id_type=MESH)

    for a, b in row_rel[1:]:
        pl.semaphore_signal(barrier, inc=1, device_id=row_peer(a, b), device_id_type=MESH)
    for rel in col_rel:
        pl.semaphore_signal(barrier, inc=1, device_id=col_peer(*rel), device_id_type=MESH)

    kgain = key_gain[...]
    keys[0:cached, :] = norm_rows(key_cache[...], kgain)
    vals[0:cached, 0:head] = value_cache[...]
    vals[:, head:] = jnp.ones((vals.shape[0], vals.shape[1] - head), bf16)
    scaled[...] = (cotangent[...].astype(f32) * out_gate[...]).astype(bf16)

    peers = len(row_rel) - 1 + len(col_rel)

    @pl.when(off_diagonal)
    def _():
        pl.semaphore_wait(barrier, peers + 1)

    @pl.when(jnp.logical_not(off_diagonal))
    def _():
        pl.semaphore_wait(barrier, peers)

    first = tok.at[0, 0, 0]
    transpose = remote(tokens, first, s_t, r_t, twin)
    stay = pltpu.make_async_copy(tokens, first, r_t)

    @pl.when(off_diagonal)
    def _():
        transpose.start()

    @pl.when(jnp.logical_not(off_diagonal))
    def _():
        stay.start()

    x_near = row_peer(1, 0)
    for i, w in enumerate((w_query, w_key, w_value)):
        send(w, wall.at[xl, :, pl.ds(i * head, head)], s_w.at[i], r_w.at[i], x_near)
        wall[xl, :, i * head : (i + 1) * head] = w[...]

    for d in order[1:]:
        send(w_out, wout.at[row], s_wo.at[slot_of[d]], r_wo.at[slot_of[(n - d) % n]], row_peer(0, d))
    wout[row] = w_out[...]
    send(w_out, wout.at[row], s_wx.at[0], r_wx.at[0], x_near)

    @pl.when(off_diagonal)
    def _():
        transpose.wait_recv()

    @pl.when(jnp.logical_not(off_diagonal))
    def _():
        stay.wait()

    def gather_start(buf, ss, rs):
        for d in reversed(order[1:]):
            i = slot_of[d]
            j = slot_of[(n - d) % n]
            send(buf.at[0, 0, 0], buf.at[0, 0, j], ss.at[0, i], rs.at[0, j], col_peer(0, d, 0))

    def gather_z(buf, ss, rs, i):
        if i:
            arrived(buf.at[0, 0, i], ss.at[0, i], rs.at[0, i])
        send(buf.at[0, 0, i], buf.at[1, 0, i], ss.at[1, i], rs.at[1, i], col_peer(1, 0, 0))
        send(buf.at[0, 0, i], buf.at[0, 1, i], ss.at[2, i], rs.at[2, i], col_peer(0, 0, 1))

    def gather_x(buf, ss, rs, i):
        arrived(buf.at[1, 0, i], ss.at[1, i], rs.at[1, i])
        send(buf.at[1, 0, i], buf.at[1, 1, i], ss.at[3, i], rs.at[3, i], col_peer(0, 0, 1))

    def gather_core(buf, ss, rs, i):
        arrived(buf.at[0, 1, i], ss.at[2, i], rs.at[2, i])
        arrived(buf.at[1, 1, i], ss.at[3, i], rs.at[3, i])

    def project(slots, lo, width):
        total = None
        lines = rows * len(slots)
        for a in (0, 1):
            for c in (0, 1):
                left = tok[a, c, slots[0] : slots[0] + len(slots)].reshape(lines, dcols)
                start = pl.multiple_of(((k + c) % 2) * dcols, 16)
                right = wall[(xh + a) % 2, pl.ds(start, dcols), lo : lo + width]
                term = jnp.dot(left, right, preferred_element_type=f32)
                total = term if total is None else total + term
        return total.astype(bf16)

    gather_start(tok, s_g, r_g)
    half = max(n // 2, 1)
    conditional = []

    def ship(i, src, dst, ssem, rsem):
        owner = (z + order[i]) % n
        copy = remote(src, dst, ssem, rsem, dev(xl, owner, xh, z, k))

        @pl.when(owner != y)
        def _():
            copy.start()

        conditional.append((owner != y, copy))

    def keep(i, dst, value):
        owner = (z + order[i]) % n

        @pl.when(owner == y)
        def _():
            dst[y] = value

    weights_here = False
    for step in range(n + 2):
        if step < n:
            gather_z(tok, s_g, r_g, step)
        if 1 <= step <= n:
            gather_x(tok, s_g, r_g, step - 1)
        if step >= 2:
            i = step - 2
            gather_core(tok, s_g, r_g, i)
            if not weights_here:
                weights_here = True
                for j in range(3):
                    part = wall.at[1 - xl, :, pl.ds(j * head, head)]
                    arrived(part, s_w.at[j], r_w.at[j])
            if (i + 1) % half == 0:
                slots = list(range(i + 1 - half, i + 1))
                product = project(slots, 0, head)
                for m, s in enumerate(slots):
                    value = product[m * rows : (m + 1) * rows]
                    qsend[s] = value
                    keep(s, qpart, value)
                    ship(s, qsend.at[s], qpart.at[y], s_q.at[s], r_q.at[y])

    for h in range(n // half):
        slots = list(range(h * half, (h + 1) * half))
        product = project(slots, head, 2 * head)
        for m, s in enumerate(slots):
            value = product[m * rows : (m + 1) * rows]
            kvsend[s] = value
            keep(s, kvpart, value)

    for i in range(1, n):
        src = (y + order[i]) % n
        arrived(wout.at[xl * n + src], s_wo.at[i], r_wo.at[i])
        send(wout.at[xl * n + src], wout.at[xl * n + src], s_wx.at[i], r_wx.at[i], x_near)

    for i in range(1, n):
        src = (y + i) % n
        arrived(qpart.at[src], s_q.at[0], r_q.at[src])
    query = qpart[0].astype(f32)
    for i in range(1, n):
        query = query + qpart[i].astype(f32)
    queries[0] = norm_rows(query.astype(bf16), query_gain[...])
    for i in range(1, 2 * n):
        j = row_inv[i]
        send(queries.at[0], queries.at[j], s_qa.at[i], r_qa.at[j], row_peer(*row_rel[i]))
    for s in range(n):
        ship(s, kvsend.at[s], kvpart.at[y], s_kv.at[s], r_kv.at[y])

    for i in range(n):
        src = (y + order[i]) % n
        arrived(wout.at[(1 - xl) * n + src], s_wx.at[i], r_wx.at[i])

    def grad_block(j, _):
        terms = lax.dot_general(scaled[...], wout[j], LAST, preferred_element_type=f32)
        for c in (0, 1):
            gsend[2 * j + c] = terms[:, c * head : (c + 1) * head].astype(bf16)
        return 0

    lax.fori_loop(0, 2 * n, grad_block, 0)
    for i, (a, b, c) in enumerate(col_rel):
        j = col_inv[i]
        _, target = col_peer(a, b, c)
        send(gsend.at[target], grecv.at[j], s_gr.at[i], r_gr.at[j], col_peer(a, b, c))

    factor = math.log2(math.e) * head ** (-0.5)
    group = max(n // 2, 1)
    n_groups = 2 * n // group
    lines = group * rows
    chunk = min(512, cached)

    def attend(g, lo, size):
        query = queries[g * group : (g + 1) * group].reshape(lines, head)
        scores = lax.dot_general(query, keys[pl.ds(lo, size), :], LAST, preferred_element_type=f32)
        weights = jnp.exp2(scores * factor).astype(bf16)
        return jnp.dot(weights, vals[pl.ds(lo, size), :], preferred_element_type=f32)

    def attend_cached(g):
        for i in range(max(g * group, 1), (g + 1) * group):
            arrived(queries.at[i], s_qa.at[i], r_qa.at[i])
        acc[g] = attend(g, 0, chunk)

        def step(i, _):
            acc[g] += attend(g, pl.multiple_of(i * chunk, chunk), chunk)
            return 0

        lax.fori_loop(1, cached // chunk, step, 0)

    same = lax.broadcasted_iota(jnp.int32, (rows, rows), 0) == lax.broadcasted_iota(
        jnp.int32, (rows, rows), 1
    )

    def attend_new(g):
        acc[g] += attend(g, cached, rows)
        for m in range(group):
            i = g * group + m
            block = acc[g, m * rows : (m + 1) * rows, :]
            total = jnp.sum(jnp.where(same, block[:, head:], 0.0), axis=0, keepdims=True)
            high = total.astype(bf16)
            low = (total - high.astype(f32)).astype(bf16)
            where = nsend.at[i] if i else nrecv.at[0]
            where[0:rows, :] = block[:, :head].astype(bf16)
            line = lax.broadcasted_iota(jnp.int32, (16, rows), 0)
            tail = jnp.where(
                line == 0,
                jnp.broadcast_to(high.astype(f32), (16, rows)),
                jnp.where(line == 1, jnp.broadcast_to(low.astype(f32), (16, rows)), 0.0),
            )
            where[rows:, :] = tail.astype(bf16)
            if i:
                j = row_inv[i]
                send(nsend.at[i], nrecv.at[j], s_n.at[i], r_n.at[j], row_peer(*row_rel[i]))

    early = n_groups // 2
    for g in range(early):
        attend_cached(g)
    for i in range(1, n):
        src = (y + i) % n
        arrived(kvpart.at[src], s_kv.at[0], r_kv.at[src])
    fresh = kvpart[0].astype(f32)
    for i in range(1, n):
        fresh = fresh + kvpart[i].astype(f32)
    fresh = fresh.astype(bf16)
    keys[cached:, :] = norm_rows(fresh[:, :head], kgain)
    vals[cached:, 0:head] = fresh[:, head:]
    for g in range(early):
        attend_new(g)
    for g in range(early, n_groups):
        attend_cached(g)
        attend_new(g)

    _, mine = col_peer(0, 0, 0)
    grad = gsend[mine].astype(f32)
    for j in range(len(col_rel)):
        arrived(grecv.at[j], s_gr.at[j], r_gr.at[j])
        grad = grad + grecv[j].astype(f32)
    grad_out[...] = grad.astype(bf16)

    for j in range(1, 2 * n):
        arrived(nrecv.at[j], s_n.at[j], r_n.at[j])
    summed = nrecv[0].astype(f32)
    for j in range(1, 2 * n):
        summed = summed + nrecv[j].astype(f32)
    total = summed[rows : rows + 1, :] + summed[rows + 1 : rows + 2, :]
    total = jnp.sum(jnp.where(same, jnp.broadcast_to(total, (rows, rows)), 0.0), axis=1, keepdims=True)
    att[0, 0, 0] = (summed[0:rows, :] / total).astype(bf16)

    gather_start(att, s_a, r_a)
    branch = jnp.zeros((rows, dcols), f32)
    for step in range(n + 2):
        if step < n:
            gather_z(att, s_a, r_a, step)
        if 1 <= step <= n:
            gather_x(att, s_a, r_a, step - 1)
        if step >= 2:
            i = step - 2
            gather_core(att, s_a, r_a, i)
            for a in (0, 1):
                chip = ((xh + a) % 2) * n + (z + order[i]) % n
                for c in (0, 1):
                    start = pl.multiple_of(((k + c) % 2) * head, 16)
                    right = wout[chip, pl.ds(start, head), :]
                    branch = branch + jnp.dot(att[a, c, i], right, preferred_element_type=f32)
    layer_out[...] = (tokens[...].astype(f32) + out_gate[...] * branch).astype(bf16)

    @pl.when(off_diagonal)
    def _():
        transpose.wait_send()

    for copy in sends:
        copy.wait_send()
    for away, copy in conditional:

        @pl.when(away)
        def _(copy=copy):
            copy.wait_send()


def body(n, *args):
    tokens, w_query, w_key, w_value, w_out, key_cache, value_cache, query_gain, key_gain, out_gate, cotangent = args
    rows, dcols = tokens.shape
    head = query_gain.shape[0]
    kin = w_query.shape[0]
    cached = key_cache.shape[0]
    group = max(n // 2, 1)
    vmem = pl.BlockSpec(memory_space=pltpu.VMEM)
    dma = pltpu.SemaphoreType.DMA
    col_peers = 4 * n - 1
    scratch = [
        pltpu.VMEM((2, 2, n, rows, dcols), bf16),
        pltpu.VMEM((2, kin, 3 * head), bf16),
        pltpu.VMEM((2 * n,) + w_out.shape, bf16),
        pltpu.VMEM((cached + rows, head), bf16),
        pltpu.VMEM((cached + rows, 2 * head), bf16),
        pltpu.VMEM((rows, dcols), bf16),
        pltpu.VMEM((n, rows, head), bf16),
        pltpu.VMEM((n, rows, head), bf16),
        pltpu.VMEM((n, rows, 2 * head), bf16),
        pltpu.VMEM((n, rows, 2 * head), bf16),
        pltpu.VMEM((2 * n, rows, head), bf16),
        pltpu.VMEM((2 * n // group, group * rows, 2 * head), f32),
        pltpu.VMEM((2 * n, rows + 16, head), bf16),
        pltpu.VMEM((2 * n, rows + 16, head), bf16),
        pltpu.VMEM((4 * n, rows, head), bf16),
        pltpu.VMEM((col_peers, rows, head), bf16),
        pltpu.VMEM((2, 2, n, rows, head), bf16),
        dma,
        dma,
        dma((3,)),
        dma((3,)),
        dma((n,)),
        dma((n,)),
        dma((n,)),
        dma((n,)),
        dma((4, n)),
        dma((4, n)),
        dma((n,)),
        dma((n,)),
        dma((n,)),
        dma((n,)),
        dma((2 * n,)),
        dma((2 * n,)),
        dma((2 * n,)),
        dma((2 * n,)),
        dma((col_peers,)),
        dma((col_peers,)),
        dma((4, n)),
        dma((4, n)),
    ]
    return pl.pallas_call(
        functools.partial(kernel, n),
        name="attention_block",
        out_shape=(
            jax.ShapeDtypeStruct((rows, dcols), bf16),
            jax.ShapeDtypeStruct((rows, head), bf16),
        ),
        in_specs=[vmem] * 11,
        out_specs=(vmem, vmem),
        scratch_shapes=scratch,
        compiler_params=pltpu.CompilerParams(
            collective_id=0, has_side_effects=True, vmem_limit_bytes=60 * 1024 * 1024
        ),
    )(
        tokens,
        w_query,
        w_key,
        w_value,
        w_out,
        key_cache,
        value_cache,
        query_gain.reshape(1, head),
        key_gain.reshape(1, head),
        out_gate.reshape(1, dcols),
        cotangent,
    )


def solution(mesh):
    n = mesh.shape["row"] // 2
    both = P("row", "col")
    placed = (both,) * 7 + (P(), P(), P("col"), both)
    return jax.shard_map(
        functools.partial(body, n),
        mesh=mesh,
        in_specs=placed,
        out_specs=(both, both),
        check_vma=False,
    )
```

time: 756 us -> 147 us (0.19)
  the two profiles are of different devices: /device:TPU:1 before, /device:TPU:9 now
where the time goes in v1:
time: 147 us; the launch traced here: 146 us
  Pallas kernels  141 us (96%)
  local copies, waits for them, and re-layouts  5.22 us (4%)
    pallas_call x1, Pallas kernels, body(): pl.pallas_call(functools.partial(kernel, n), name='attention_block', out_...  141 us
    unnamed x10, local copies, waits for them, and re-layouts  3.66 us

profile of v1, /device:TPU:9, one launch (start us, length us, event | category | flops | bytes accessed | tf_op | source)
XLA Modules:
  0.0 146.5 jit_solution(563554285405098540)
XLA Ops:
  0.6 0.0 copy-start.1
  0.6 0.0 copy-start
  0.6 1.6 %copy.13.tokens = bf16[128,192]{1,0:T(8,128)(2,1)} copy(bf16[128,192]{0,1:T(8,128)(2,1)} %param.11) | data formatting | bytes 98304 | tf_op args[0]
  2.2 0.0 copy-done.1
  2.2 0.7 copy.15.cotangent
  2.9 0.0 copy-done
  2.9 0.7 copy.14.w_out
  3.7 140.6 %attention_block.1 = (bf16[128,192]{1,0:T(8,128)(2,1)}, bf16[128,128]{1,0:T(8,128)(2,1)}) custom-call(bf16[128,192]{1,0:T(8,128)(2,1)} %copy.13.tokens, bf16[384,128]{1,0:T(8,128)(2,1)} %w_query.1, bf16[384,128]{1,0:T(8,128)(2,1)} %w_key.1, bf16[384,128]{1,0:T(8,128)(2,1)} %w_value.1, bf16[256,192]{1,0:T(8,128)(2,1)} %copy.14.w_out, ...), custom_call_target="tpu_custom_call" | custom-call | tf_op jit(solution)/shard_map/attention_block/pallas_call | solution.py:480
  144.3 0.0 copy-start.2
  144.3 1.6 %copy.16 = bf16[128,192]{0,1:T(8,128)(2,1)} copy(bf16[128,192]{1,0:T(8,128)(2,1)} %get-tuple-element.2) | data formatting | bytes 98304 | tf_op jit(solution)/shard_map/attention_block/pallas_call | solution.py:480
  145.9 0.0 copy-done.2
  145.9 0.6 copy.18
Async XLA Ops:
  0.6 1.6 %copy-start.1 = (bf16[128,192]{0,1:T(8,128)(2,1)S(1)}, bf16[128,192]{0,1:T(8,128)(2,1)}, u32[]{:S(2)}) copy-start(bf16[128,192]{0,1:T(8,128)(2,1)} %param.21) | copy-start | bytes 147460
  0.6 2.3 %copy-start = (bf16[256,192]{0,1:T(8,128)(2,1)S(1)}, bf16[256,192]{0,1:T(8,128)(2,1)}, u32[]{:S(2)}) copy-start(bf16[256,192]{0,1:T(8,128)(2,1)} %param.15) | copy-start | bytes 294916
  144.3 1.6 %copy-start.2 = (bf16[128,128]{1,0:T(8,128)(2,1)S(1)}, bf16[128,128]{1,0:T(8,128)(2,1)}, u32[]{:S(2)}) copy-start(bf16[128,128]{1,0:T(8,128)(2,1)} %get-tuple-element.7) | copy-start | bytes 98308

commit v2 on v1

v2 whole, which is shorter than its diff:
```python
import functools
import math

import jax
import jax.numpy as jnp
from jax import lax
from jax.experimental import pallas as pl
from jax.experimental.pallas import tpu as pltpu
from jax.sharding import PartitionSpec as P

MESH = pl.DeviceIdType.MESH
epsilon = 1e-06
f32 = jnp.float32
bf16 = jnp.bfloat16
FIRST = (((0,), (0,)), ((), ()))
LAST = (((1,), (1,)), ((), ()))


def norm_rows(values, gain):
    wide = values.astype(f32)
    mean_square = jnp.mean(wide * wide, axis=-1, keepdims=True)
    return (wide * lax.rsqrt(mean_square + epsilon) * gain).astype(bf16)


def ring_order(n):
    order = [0]
    for d in range(1, n // 2 + 1):
        order.append(d)
        if (n - d) % n != d:
            order.append(n - d)
    return order


def kernel(
    n,
    tokens,
    w_query,
    w_key,
    w_value,
    w_out,
    key_cache,
    value_cache,
    query_gain,
    key_gain,
    out_gate,
    cotangent,
    layer_out,
    grad_out,
    tok,
    wall,
    wout,
    keys,
    vals,
    scaled,
    qsend,
    qpart,
    kvsend,
    kvpart,
    queries,
    acc,
    nsend,
    nrecv,
    gsend,
    gpair,
    gsum,
    grecv,
    att,
    kraw,
    tokv,
    cotv,
    s_in,
    s_t,
    r_t,
    s_w,
    r_w,
    s_wo,
    r_wo,
    s_wx,
    r_wx,
    s_g,
    r_g,
    s_q,
    r_q,
    s_kv,
    r_kv,
    s_qa,
    r_qa,
    s_n,
    r_n,
    s_gp,
    r_gp,
    s_gr,
    r_gr,
    s_a,
    r_a,
):
    dcols, rows = tokens.shape
    head = query_gain.shape[1]
    cached = key_cache.shape[0]
    row = lax.axis_index("row")
    col = lax.axis_index("col")
    xl, y = row // n, row % n
    xh, z, k = col // (2 * n), (col // 2) % n, col % 2

    def dev(xl_, y_, xh_, z_, k_):
        return (xl_ * n + y_, (xh_ * n + z_) * 2 + k_)

    order = ring_order(n)
    slot_of = {d: i for i, d in enumerate(order)}

    group = max(n // 2, 1)
    near, far = order[:group], order[group:]
    row_rel = [(0, b) for b in near + far] + [(1, b) for b in near + far]
    row_inv = [row_rel.index((a, (n - b) % n)) for a, b in row_rel]
    own = row_rel.index((0, 0))
    others = [i for i in range(2 * n) if i != own]
    if n == 8:
        hops = {0: ((2, None), (6, None), (1, None), (7, None))}
        hops[2] = ((7, None), (6, 0))
        hops[6] = ((1, None), (2, 1))
        turns = [slot_of[d] for d in (0, 2, 6, 1, 7, 3, 5, 4)]
    else:
        hops = {0: tuple((d, None) for d in range(1, n))}
        turns = list(range(n))
    chip_rel = [(a, b) for b in order for a in (0, 1)]
    chip_inv = [chip_rel.index((a, (n - b) % n)) for a, b in chip_rel]
    col_rel = [
        (a, b, c)
        for b in order
        for a in (0, 1)
        for c in (0, 1)
        if (a, b, c) != (0, 0, 0)
    ]

    def row_peer(a, b):
        return dev((xl + a) % 2, (y + b) % n, xh, z, k)

    def col_peer(a, b, c):
        return dev(xl, y, (xh + a) % 2, (z + b) % n, (k + c) % 2)

    def remote(src, dst, ssem, rsem, to):
        return pltpu.make_async_remote_copy(
            src_ref=src, dst_ref=dst, send_sem=ssem, recv_sem=rsem, device_id=to, device_id_type=MESH
        )

    any_peer = col_peer(0, 0, 1)

    def arrived(dst, ssem, rsem):
        remote(dst, dst, ssem, rsem, any_peer).wait_recv()

    sends = []

    def send(src, dst, ssem, rsem, to):
        copy = remote(src, dst, ssem, rsem, to)
        copy.start()
        sends.append(copy)

    barrier = pltpu.get_barrier_semaphore()
    off_diagonal = y != z
    twin = dev(xl, z, xh, y, k)

    @pl.when(off_diagonal)
    def _():
        pl.semaphore_signal(barrier, inc=1, device_id=twin, device_id_type=MESH)

    for i in others:
        pl.semaphore_signal(barrier, inc=1, device_id=row_peer(*row_rel[i]), device_id_type=MESH)
    for rel in col_rel:
        pl.semaphore_signal(barrier, inc=1, device_id=col_peer(*rel), device_id_type=MESH)

    local = [
        (key_cache, kraw),
        (cotangent, cotv),
        (value_cache, vals.at[pl.ds(0, cached), pl.ds(0, head)]),
        (w_query, wall.at[xl, :, pl.ds(0, head)]),
        (w_key, wall.at[xl, :, pl.ds(head, head)]),
        (w_value, wall.at[xl, :, pl.ds(2 * head, head)]),
        (w_out, wout.at[row]),
        (tokens, tokv),
    ]
    loads = [pltpu.make_async_copy(src, dst, s_in.at[i]) for i, (src, dst) in enumerate(local)]
    for load in loads:
        load.start()
    vals[:, head:] = jnp.ones((vals.shape[0], vals.shape[1] - head), bf16)
    kgain = key_gain[...]
    gate = jnp.transpose(jnp.broadcast_to(out_gate[...], (rows, dcols)))
    loads[0].wait()
    keys[0:cached, :] = norm_rows(kraw[...], kgain)
    loads[1].wait()
    scaled[...] = jnp.transpose((cotv[...].astype(f32) * gate).astype(bf16))
    for load in loads[2:]:
        load.wait()

    peers = len(row_rel) - 1 + len(col_rel)

    @pl.when(off_diagonal)
    def _():
        pl.semaphore_wait(barrier, peers + 1)

    @pl.when(jnp.logical_not(off_diagonal))
    def _():
        pl.semaphore_wait(barrier, peers)

    first = tok.at[0, 2 * xh + k]
    transpose = remote(tokens, first, s_t, r_t, twin)
    stay = pltpu.make_async_copy(tokens, first, r_t)

    @pl.when(off_diagonal)
    def _():
        transpose.start()

    @pl.when(jnp.logical_not(off_diagonal))
    def _():
        stay.start()

    x_near = row_peer(1, 0)
    for i, w in enumerate((w_query, w_key, w_value)):
        send(w, wall.at[xl, :, pl.ds(i * head, head)], s_w.at[i], r_w.at[i], x_near)


    def pass_weights(*slots):
        for i in slots:
            if i < n:
                block = wout.at[xl * n + (y + order[i]) % n]
                arrived(block, s_wo.at[i], r_wo.at[i])
                send(block, block, s_wx.at[i], r_wx.at[i], x_near)

    @pl.when(off_diagonal)
    def _():
        transpose.wait_recv()

    @pl.when(jnp.logical_not(off_diagonal))
    def _():
        stay.wait()

    def place(a, c):
        return ((xh + a) % 2) * 2 + (k + c) % 2

    def relay(buf, ss, rs, a, d):
        block = buf.at[slot_of[d], place(a, 0)]
        for step, only in hops.get(d, ()):
            if only is None or only == a:
                j = slot_of[(d - step) % n]
                send(block, buf.at[j, place(a, 0)], ss.at[a, j], rs.at[a, j], col_peer(0, step, 0))

    def share(buf, ss, rs, a, i):
        block = buf.at[i, place(a, 0)]
        send(block, block, ss.at[2 + a, i], rs.at[2 + a, i], col_peer(0, 0, 1))

    def gather_start(buf, ss, rs):
        block = buf.at[0, place(0, 0)]
        send(block, block, ss.at[1, 0], rs.at[1, 0], col_peer(1, 0, 0))
        relay(buf, ss, rs, 0, 0)
        share(buf, ss, rs, 0, 0)

    def gather_other(buf, ss, rs):
        arrived(buf.at[0, place(1, 0)], ss.at[1, 0], rs.at[1, 0])
        relay(buf, ss, rs, 1, 0)
        share(buf, ss, rs, 1, 0)

    def gather_z(buf, ss, rs, i):
        if i:
            for a in (0, 1):
                arrived(buf.at[i, place(a, 0)], ss.at[a, i], rs.at[a, i])
                relay(buf, ss, rs, a, order[i])
                share(buf, ss, rs, a, i)

    def gather_core(buf, ss, rs, i):
        for a in (0, 1):
            arrived(buf.at[i, place(a, 1)], ss.at[2 + a, i], rs.at[2 + a, i])

    lag = 2

    def project(slot, lo, width):
        left = tok[slot].reshape(4 * dcols, rows)
        right = wall[:, :, lo : lo + width].reshape(4 * dcols, width)
        return lax.dot_general(left, right, FIRST, preferred_element_type=f32).astype(bf16)

    gather_start(tok, s_g, r_g)
    for d in order[1:]:
        send(w_out, wout.at[row], s_wo.at[slot_of[d]], r_wo.at[slot_of[(n - d) % n]], row_peer(0, d))
    gather_other(tok, s_g, r_g)
    send(w_out, wout.at[row], s_wx.at[0], r_wx.at[0], x_near)
    weights_here = False
    for step in range(n + lag):
        if step < n:
            gather_z(tok, s_g, r_g, turns[step])
        if step >= lag:
            i = turns[step - lag]
            gather_core(tok, s_g, r_g, i)
            if not weights_here:
                weights_here = True
                for j in range(3):
                    part = wall.at[1 - xl, :, pl.ds(j * head, head)]
                    arrived(part, s_w.at[j], r_w.at[j])
            value = project(i, 0, 3 * head)
            owner = (z + order[i]) % n
            qsend[owner] = value[:, :head]
            kvsend[owner] = value[:, head:]
    for d in reversed(order[1:]):
        owner = (y + d) % n
        send(qsend.at[owner], qpart.at[y], s_q.at[d], r_q.at[y], row_peer(0, d))
    qpart[y] = qsend[y]
    kvpart[y] = kvsend[y]
    pass_weights(*range(1, n))

    for i in range(1, n):
        src = (y + i) % n
        arrived(qpart.at[src], s_q.at[0], r_q.at[src])
    query = qpart[0].astype(f32)
    for i in range(1, n):
        query = query + qpart[i].astype(f32)
    queries[own] = norm_rows(query.astype(bf16), query_gain[...])
    send(queries.at[own], queries.at[n], s_qa.at[n], r_qa.at[n], x_near)
    for d in order[1:]:
        i = slot_of[d]
        j = slot_of[n - d]
        send(queries.at[own], queries.at[j], s_qa.at[i], r_qa.at[j], row_peer(0, d))
    for d in reversed(order[1:]):
        owner = (y + d) % n
        send(kvsend.at[owner], kvpart.at[y], s_kv.at[d], r_kv.at[y], row_peer(0, d))

    def grad_block(j, _):
        terms = jnp.dot(scaled[...], wout[j], preferred_element_type=f32)
        for c in (0, 1):
            gsend[c, j] = terms[:, c * head : (c + 1) * head].astype(bf16)
        return 0

    def grad_terms():
        for i in range(n):
            src = (y + order[i]) % n
            arrived(wout.at[(1 - xl) * n + src], s_wx.at[i], r_wx.at[i])

        lax.fori_loop(0, 2 * n, grad_block, 0)
        send(gsend.at[1 - k], gpair, s_gp, r_gp, col_peer(0, 0, 1))

    def grad_send():
        arrived(gpair, s_gp, r_gp)
        gsum[...] = (gsend[k].astype(f32) + gpair[...].astype(f32)).astype(bf16)
        for i, (a, b) in enumerate(chip_rel):
            if i:
                chip = ((xh + a) % 2) * n + (z + b) % n
                j = chip_inv[i]
                send(gsum.at[chip], grecv.at[j], s_gr.at[i], r_gr.at[j], col_peer(a, b, 0))

    factor = math.log2(math.e) * head ** (-0.5)
    n_groups = 2 * n // group
    lines = group * rows
    chunk = min(512, cached)

    def attend(g, lo, size):
        query = queries[g * group : (g + 1) * group].reshape(lines, head)
        scores = lax.dot_general(query, keys[pl.ds(lo, size), :], LAST, preferred_element_type=f32)
        weights = jnp.exp2(scores * factor).astype(bf16)
        return jnp.dot(weights, vals[pl.ds(lo, size), :], preferred_element_type=f32)

    def attend_cached(g):
        for i in range(g * group, (g + 1) * group):
            if i == own:
                continue
            arrived(queries.at[i], s_qa.at[i], r_qa.at[i])
            if i < n:
                send(queries.at[i], queries.at[n + i], s_qa.at[n + i], r_qa.at[n + i], x_near)
        acc[g] = attend(g, 0, chunk)

        def step(i, _):
            acc[g] += attend(g, pl.multiple_of(i * chunk, chunk), chunk)
            return 0

        lax.fori_loop(1, cached // chunk, step, 0)

    same = lax.broadcasted_iota(jnp.int32, (rows, rows), 0) == lax.broadcasted_iota(
        jnp.int32, (rows, rows), 1
    )

    line = lax.broadcasted_iota(jnp.int32, (16, rows), 0)

    def pack(where, numer, total):
        high = total.astype(bf16).astype(f32)
        low = total - high
        where[0:rows, :] = numer.astype(bf16)
        high, low = jnp.broadcast_to(high, (16, rows)), jnp.broadcast_to(low, (16, rows))
        where[rows:, :] = jnp.where(line == 0, high, jnp.where(line == 1, low, 0.0)).astype(bf16)

    def attend_new(g):
        acc[g] += attend(g, cached, rows)
        for m in range(group):
            i = g * group + m
            block = acc[g, m * rows : (m + 1) * rows, :]
            total = jnp.sum(jnp.where(same, block[:, head:], 0.0), axis=0, keepdims=True)
            if i == own:
                pack(nrecv.at[own], block[:, :head], total)
            else:
                pack(nsend.at[i], block[:, :head], total)
                j = row_inv[i]
                send(nsend.at[i], nrecv.at[j], s_n.at[i], r_n.at[j], row_peer(*row_rel[i]))

    attend_cached(0)
    grad_terms()
    attend_cached(1)
    attend_cached(2)
    grad_send()
    attend_cached(3)
    for i in range(1, n):
        src = (y + i) % n
        arrived(kvpart.at[src], s_kv.at[0], r_kv.at[src])
    fresh = kvpart[0].astype(f32)
    for i in range(1, n):
        fresh = fresh + kvpart[i].astype(f32)
    fresh = fresh.astype(bf16)
    keys[cached:, :] = norm_rows(fresh[:, :head], kgain)
    vals[cached:, 0:head] = fresh[:, head:]
    for g in range(4):
        attend_new(g)

    for j in others:
        arrived(nrecv.at[j], s_n.at[j], r_n.at[j])
    summed = nrecv[own].astype(f32)
    for j in others:
        summed = summed + nrecv[j].astype(f32)
    total = summed[rows : rows + 1, :] + summed[rows + 1 : rows + 2, :]
    att[0, place(0, 0)] = (jnp.transpose(summed[0:rows, :]) / total).astype(bf16)

    gather_start(att, s_a, r_a)
    gather_other(att, s_a, r_a)
    grad = gsum[xh * n + z].astype(f32)
    for j in range(1, 2 * n):
        arrived(grecv.at[j], s_gr.at[j], r_gr.at[j])
        grad = grad + grecv[j].astype(f32)
    grad_out[...] = grad.astype(bf16)
    branch = jnp.zeros((dcols, rows), f32)
    for step in range(n + lag):
        if step < n:
            gather_z(att, s_a, r_a, turns[step])
        if step >= lag:
            i = turns[step - lag]
            gather_core(att, s_a, r_a, i)
            for a in (0, 1):
                right = att[i, 2 * a : 2 * a + 2].reshape(2 * head, rows)
                left = wout[a * n + (z + order[i]) % n]
                branch = branch + jnp.dot(left, right, preferred_element_type=f32)
    gate = jnp.transpose(jnp.broadcast_to(out_gate[...], (rows, dcols)))
    layer_out[...] = (tokv[...].astype(f32) + gate * branch).astype(bf16)

    @pl.when(off_diagonal)
    def _():
        transpose.wait_send()

    for copy in sends:
        copy.wait_send()


def body(n, *args):
    tokens, w_query, w_key, w_value, w_out, key_cache, value_cache, query_gain, key_gain, out_gate, cotangent = args
    rows, dcols = tokens.shape
    flipped = (w_out.shape[1], w_out.shape[0])
    head = query_gain.shape[0]
    kin = w_query.shape[0]
    cached = key_cache.shape[0]
    group = max(n // 2, 1)
    vmem = pl.BlockSpec(memory_space=pltpu.VMEM)
    hbm = pl.BlockSpec(memory_space=pl.ANY)
    dma = pltpu.SemaphoreType.DMA
    scratch = [
        pltpu.VMEM((n, 4, dcols, rows), bf16),
        pltpu.VMEM((2, kin, 3 * head), bf16),
        pltpu.VMEM((2 * n,) + flipped, bf16),
        pltpu.VMEM((cached + rows, head), bf16),
        pltpu.VMEM((cached + rows, 2 * head), bf16),
        pltpu.VMEM((rows, dcols), bf16),
        pltpu.VMEM((n, rows, head), bf16),
        pltpu.VMEM((n, rows, head), bf16),
        pltpu.VMEM((n, rows, 2 * head), bf16),
        pltpu.VMEM((n, rows, 2 * head), bf16),
        pltpu.VMEM((2 * n, rows, head), bf16),
        pltpu.VMEM((2 * n // group, group * rows, 2 * head), f32),
        pltpu.VMEM((2 * n, rows + 16, head), bf16),
        pltpu.VMEM((2 * n, rows + 16, head), bf16),
        pltpu.VMEM((2, 2 * n, rows, head), bf16),
        pltpu.VMEM((2 * n, rows, head), bf16),
        pltpu.VMEM((2 * n, rows, head), bf16),
        pltpu.VMEM((2 * n, rows, head), bf16),
        pltpu.VMEM((n, 4, head, rows), bf16),
        pltpu.VMEM((cached, head), bf16),
        pltpu.VMEM((dcols, rows), bf16),
        pltpu.VMEM((dcols, rows), bf16),
        dma((8,)),
        dma,
        dma,
        dma((3,)),
        dma((3,)),
        dma((n,)),
        dma((n,)),
        dma((n,)),
        dma((n,)),
        dma((4, n)),
        dma((4, n)),
        dma((n,)),
        dma((n,)),
        dma((n,)),
        dma((n,)),
        dma((2 * n,)),
        dma((2 * n,)),
        dma((2 * n,)),
        dma((2 * n,)),
        dma,
        dma,
        dma((2 * n,)),
        dma((2 * n,)),
        dma((4, n)),
        dma((4, n)),
    ]
    layer_out, grad = pl.pallas_call(
        functools.partial(kernel, n),
        name="attention_block",
        out_shape=(
            jax.ShapeDtypeStruct((dcols, rows), bf16),
            jax.ShapeDtypeStruct((rows, head), bf16),
        ),
        in_specs=[hbm] * 7 + [vmem] * 3 + [hbm],
        out_specs=(vmem, vmem),
        scratch_shapes=scratch,
        compiler_params=pltpu.CompilerParams(
            collective_id=0, has_side_effects=True, vmem_limit_bytes=60 * 1024 * 1024
        ),
    )(
        tokens.T,
        w_query,
        w_key,
        w_value,
        w_out.T,
        key_cache,
        value_cache,
        query_gain.reshape(1, head),
        key_gain.reshape(1, head),
        out_gate.reshape(1, dcols),
        cotangent.T,
    )
    return layer_out.T, grad


def solution(mesh):
    n = mesh.shape["row"] // 2
    both = P("row", "col")
    placed = (both,) * 7 + (P(), P(), P("col"), both)
    return jax.shard_map(
        functools.partial(body, n),
        mesh=mesh,
        in_specs=placed,
        out_specs=(both, both),
        check_vma=False,
    )
```

time: 147 us -> 106 us (0.72)
  the two profiles are of different devices: /device:TPU:9 before, /device:TPU:1 now
where the time goes in v2:
time: 106 us
  Pallas kernels  103 us (97%)
  local copies, waits for them, and re-layouts  2.05 us (2%)
    pallas_call x1, Pallas kernels, body(): pl.pallas_call(functools.partial(kernel, n), name='attention_block', out_...  103 us

profile of v2, /device:TPU:1, one launch (start us, length us, event | category | flops | bytes accessed | tf_op | source)
XLA Modules:
  0.0 105.9 jit_solution(16404147895556450779)
XLA Ops:
  0.6 103.2 %attention_block.1 = (bf16[192,128]{1,0:T(8,128)(2,1)}, bf16[128,128]{1,0:T(8,128)(2,1)}) custom-call(bf16[192,128]{1,0:T(8,128)(2,1)} %bitcast.8, bf16[384,128]{1,0:T(8,128)(2,1)} %w_query.1, bf16[384,128]{1,0:T(8,128)(2,1)} %w_key.1, bf16[384,128]{1,0:T(8,128)(2,1)} %w_value.1, bf16[192,256]{1,0:T(8,128)(2,1)} %bitcast.7, bf16[2048,128]{1,0:T(8,128)(2,1)} %key_cache.1, ...), custom_call_target="tpu_custom_call" | custom-call | tf_op jit(solution)/shard_map/attention_block/pallas_call | solution.py:513
  103.8 0.0 copy-start
  103.8 1.4 %copy.15 = bf16[128,192]{0,1:T(8,128)(2,1)} copy(bf16[128,192]{0,1:T(8,128)(2,1)} %bitcast.10) | data formatting | bytes 98304
  105.3 0.0 copy-done
  105.3 0.6 copy.16
Async XLA Ops:
  103.8 1.4 %copy-start = (bf16[128,128]{1,0:T(8,128)(2,1)S(1)}, bf16[128,128]{1,0:T(8,128)(2,1)}, u32[]{:S(2)}) copy-start(bf16[128,128]{1,0:T(8,128)(2,1)} %get-tuple-element.9) | copy-start | bytes 98308

commit v3 on v2

--- a/solution.py
+++ b/solution.py
@@ -60,6 +60,7 @@
     acc,
     nsend,
     nrecv,
+    nside,
     gsend,
     gpair,
     gsum,
@@ -87,6 +88,7 @@
     r_qa,
     s_n,
     r_n,
+    r_nx,
     s_gp,
     r_gp,
     s_gr,
@@ -118,7 +120,7 @@
         hops = {0: ((2, None), (6, None), (1, None), (7, None))}
         hops[2] = ((7, None), (6, 0))
         hops[6] = ((1, None), (2, 1))
-        turns = [slot_of[d] for d in (0, 2, 6, 1, 7, 3, 5, 4)]
+        turns = [slot_of[d] for d in (2, 6, 0, 1, 7, 3, 5, 4)]
     else:
         hops = {0: tuple((d, None) for d in range(1, n))}
         turns = list(range(n))
@@ -223,6 +225,10 @@
             if i < n:
                 block = wout.at[xl * n + (y + order[i]) % n]
                 arrived(block, s_wo.at[i], r_wo.at[i])
+                for step, only in hops.get(order[i], ()):
+                    if not only:
+                        j = slot_of[(order[i] - step) % n]
+                        send(block, block, s_wo.at[j], r_wo.at[j], row_peer(0, step))
                 send(block, block, s_wx.at[i], r_wx.at[i], x_near)
 
     @pl.when(off_diagonal)
@@ -249,20 +255,23 @@
 
     def gather_start(buf, ss, rs):
         block = buf.at[0, place(0, 0)]
+        for step, _ in hops[0][:2]:
+            j = slot_of[(n - step) % n]
+            for a in (0, 1):
+                send(block, buf.at[j, place(0, 0)], ss.at[a, j], rs.at[a, j], col_peer(a, step, 0))
         send(block, block, ss.at[1, 0], rs.at[1, 0], col_peer(1, 0, 0))
-        relay(buf, ss, rs, 0, 0)
+        for step, _ in hops[0][2:]:
+            j = slot_of[(n - step) % n]
+            for a in (0, 1):
+                send(block, buf.at[j, place(0, 0)], ss.at[a, j], rs.at[a, j], col_peer(a, step, 0))
         share(buf, ss, rs, 0, 0)
 
-    def gather_other(buf, ss, rs):
-        arrived(buf.at[0, place(1, 0)], ss.at[1, 0], rs.at[1, 0])
-        relay(buf, ss, rs, 1, 0)
-        share(buf, ss, rs, 1, 0)
-
     def gather_z(buf, ss, rs, i):
-        if i:
-            for a in (0, 1):
+        for a in (0, 1):
+            if i or a:
                 arrived(buf.at[i, place(a, 0)], ss.at[a, i], rs.at[a, i])
-                relay(buf, ss, rs, a, order[i])
+                if i:
+                    relay(buf, ss, rs, a, order[i])
                 share(buf, ss, rs, a, i)
 
     def gather_core(buf, ss, rs, i):
@@ -277,14 +286,16 @@
         return lax.dot_general(left, right, FIRST, preferred_element_type=f32).astype(bf16)
 
     gather_start(tok, s_g, r_g)
-    for d in order[1:]:
-        send(w_out, wout.at[row], s_wo.at[slot_of[d]], r_wo.at[slot_of[(n - d) % n]], row_peer(0, d))
-    gather_other(tok, s_g, r_g)
+    for step, _ in hops[0]:
+        j = slot_of[(n - step) % n]
+        send(w_out, wout.at[row], s_wo.at[j], r_wo.at[j], row_peer(0, step))
     send(w_out, wout.at[row], s_wx.at[0], r_wx.at[0], x_near)
     weights_here = False
     for step in range(n + lag):
         if step < n:
             gather_z(tok, s_g, r_g, turns[step])
+        if step == 2:
+            pass_weights(3, 4)
         if step >= lag:
             i = turns[step - lag]
             gather_core(tok, s_g, r_g, i)
@@ -302,7 +313,7 @@
         send(qsend.at[owner], qpart.at[y], s_q.at[d], r_q.at[y], row_peer(0, d))
     qpart[y] = qsend[y]
     kvpart[y] = kvsend[y]
-    pass_weights(*range(1, n))
+    pass_weights(1, 2, *range(5, n))
 
     for i in range(1, n):
         src = (y + i) % n
@@ -386,20 +397,31 @@
         acc[g] += attend(g, cached, rows)
         for m in range(group):
             i = g * group + m
+            a, b = row_rel[i]
+            t = slot_of[b]
             block = acc[g, m * rows : (m + 1) * rows, :]
+            numer = block[:, :head]
             total = jnp.sum(jnp.where(same, block[:, head:], 0.0), axis=0, keepdims=True)
+            if a:
+                pack(nsend.at[i], numer, total)
+                send(nsend.at[i], nside.at[t], s_n.at[i], r_nx.at[t], x_near)
+                continue
+            arrived(nside.at[t], s_n.at[i], r_nx.at[t])
+            side = nside[t].astype(f32)
+            numer = numer + side[0:rows, :]
+            total = total + side[rows : rows + 1, :] + side[rows + 1 : rows + 2, :]
             if i == own:
-                pack(nrecv.at[own], block[:, :head], total)
+                pack(nrecv.at[own], numer, total)
             else:
-                pack(nsend.at[i], block[:, :head], total)
+                pack(nsend.at[i], numer, total)
                 j = row_inv[i]
-                send(nsend.at[i], nrecv.at[j], s_n.at[i], r_n.at[j], row_peer(*row_rel[i]))
-
+                send(nsend.at[i], nrecv.at[j], s_n.at[i], r_n.at[j], row_peer(0, b))
+
+    grad_terms()
     attend_cached(0)
-    grad_terms()
+    grad_send()
     attend_cached(1)
     attend_cached(2)
-    grad_send()
     attend_cached(3)
     for i in range(1, n):
         src = (y + i) % n
@@ -410,19 +432,18 @@
     fresh = fresh.astype(bf16)
     keys[cached:, :] = norm_rows(fresh[:, :head], kgain)
     vals[cached:, 0:head] = fresh[:, head:]
-    for g in range(4):
+    for g in (3, 2, 1, 0):
         attend_new(g)
 
-    for j in others:
+    for j in range(1, n):
         arrived(nrecv.at[j], s_n.at[j], r_n.at[j])
     summed = nrecv[own].astype(f32)
-    for j in others:
+    for j in range(1, n):
         summed = summed + nrecv[j].astype(f32)
     total = summed[rows : rows + 1, :] + summed[rows + 1 : rows + 2, :]
     att[0, place(0, 0)] = (jnp.transpose(summed[0:rows, :]) / total).astype(bf16)
 
     gather_start(att, s_a, r_a)
-    gather_other(att, s_a, r_a)
     grad = gsum[xh * n + z].astype(f32)
     for j in range(1, 2 * n):
         arrived(grecv.at[j], s_gr.at[j], r_gr.at[j])
@@ -475,7 +496,8 @@
         pltpu.VMEM((2 * n, rows, head), bf16),
         pltpu.VMEM((2 * n // group, group * rows, 2 * head), f32),
         pltpu.VMEM((2 * n, rows + 16, head), bf16),
-        pltpu.VMEM((2 * n, rows + 16, head), bf16),
+        pltpu.VMEM((n, rows + 16, head), bf16),
+        pltpu.VMEM((n, rows + 16, head), bf16),
         pltpu.VMEM((2, 2 * n, rows, head), bf16),
         pltpu.VMEM((2 * n, rows, head), bf16),
         pltpu.VMEM((2 * n, rows, head), bf16),
@@ -502,7 +524,8 @@
         dma((2 * n,)),
         dma((2 * n,)),
         dma((2 * n,)),
-        dma((2 * n,)),
+        dma((n,)),
+        dma((n,)),
         dma,
         dma,
         dma((2 * n,)),

time: 106 us -> 100 us (0.943)
  Pallas kernels: 103 us -> 97.3 us
    pallas_call x1, Pallas kernels: 103 us -> 97.3 us  [body(): pl.pallas_call(functools.partial(kernel, n), name='attention_block', out_...]
where the time goes in v3:
time: 100 us
  Pallas kernels  97.3 us (97%)
  local copies, waits for them, and re-layouts  2.05 us (2%)
    pallas_call x1, Pallas kernels, body(): pl.pallas_call(functools.partial(kernel, n), name='attention_block', out_...  97.3 us
    unnamed x4, local copies, waits for them, and re-layouts  2.05 us

profile of v3, /device:TPU:1, one launch (start us, length us, event | category | flops | bytes accessed | tf_op | source)
XLA Modules:
  0.0 100.0 jit_solution(8273287709697418507)
XLA Ops:
  0.6 97.3 %attention_block.1 = (bf16[192,128]{1,0:T(8,128)(2,1)}, bf16[128,128]{1,0:T(8,128)(2,1)}) custom-call(bf16[192,128]{1,0:T(8,128)(2,1)} %bitcast.8, bf16[384,128]{1,0:T(8,128)(2,1)} %w_query.1, bf16[384,128]{1,0:T(8,128)(2,1)} %w_key.1, bf16[384,128]{1,0:T(8,128)(2,1)} %w_value.1, bf16[192,256]{1,0:T(8,128)(2,1)} %bitcast.7, bf16[2048,128]{1,0:T(8,128)(2,1)} %key_cache.1, ...), custom_call_target="tpu_custom_call" | custom-call | tf_op jit(solution)/shard_map/attention_block/pallas_call | solution.py:536
  97.9 0.0 copy-start
  97.9 1.4 %copy.15 = bf16[128,192]{0,1:T(8,128)(2,1)} copy(bf16[128,192]{0,1:T(8,128)(2,1)} %bitcast.10) | data formatting | bytes 98304
  99.3 0.0 copy-done
  99.4 0.6 copy.16
Async XLA Ops:
  97.9 1.4 %copy-start = (bf16[128,128]{1,0:T(8,128)(2,1)S(1)}, bf16[128,128]{1,0:T(8,128)(2,1)}, u32[]{:S(2)}) copy-start(bf16[128,128]{1,0:T(8,128)(2,1)} %get-tuple-element.9) | copy-start | bytes 98308

commit v4 on v3

--- a/solution.py
+++ b/solution.py
@@ -296,6 +296,8 @@
             gather_z(tok, s_g, r_g, turns[step])
         if step == 2:
             pass_weights(3, 4)
+        if step == 5:
+            pass_weights(1, 2)
         if step >= lag:
             i = turns[step - lag]
             gather_core(tok, s_g, r_g, i)
@@ -313,7 +315,9 @@
         send(qsend.at[owner], qpart.at[y], s_q.at[d], r_q.at[y], row_peer(0, d))
     qpart[y] = qsend[y]
     kvpart[y] = kvsend[y]
-    pass_weights(1, 2, *range(5, n))
+    if n < 5:
+        pass_weights(1, 2)
+    pass_weights(*range(5, n))
 
     for i in range(1, n):
         src = (y + i) % n
@@ -321,15 +325,13 @@
     query = qpart[0].astype(f32)
     for i in range(1, n):
         query = query + qpart[i].astype(f32)
-    queries[own] = norm_rows(query.astype(bf16), query_gain[...])
+    factor = math.log2(math.e) * head ** (-0.5)
+    queries[own] = norm_rows(query.astype(bf16), query_gain[...] * factor)
     send(queries.at[own], queries.at[n], s_qa.at[n], r_qa.at[n], x_near)
     for d in order[1:]:
         i = slot_of[d]
         j = slot_of[n - d]
         send(queries.at[own], queries.at[j], s_qa.at[i], r_qa.at[j], row_peer(0, d))
-    for d in reversed(order[1:]):
-        owner = (y + d) % n
-        send(kvsend.at[owner], kvpart.at[y], s_kv.at[d], r_kv.at[y], row_peer(0, d))
 
     def grad_block(j, _):
         terms = jnp.dot(scaled[...], wout[j], preferred_element_type=f32)
@@ -354,7 +356,6 @@
                 j = chip_inv[i]
                 send(gsum.at[chip], grecv.at[j], s_gr.at[i], r_gr.at[j], col_peer(a, b, 0))
 
-    factor = math.log2(math.e) * head ** (-0.5)
     n_groups = 2 * n // group
     lines = group * rows
     chunk = min(512, cached)
@@ -362,7 +363,7 @@
     def attend(g, lo, size):
         query = queries[g * group : (g + 1) * group].reshape(lines, head)
         scores = lax.dot_general(query, keys[pl.ds(lo, size), :], LAST, preferred_element_type=f32)
-        weights = jnp.exp2(scores * factor).astype(bf16)
+        weights = jnp.exp2(scores).astype(bf16)
         return jnp.dot(weights, vals[pl.ds(lo, size), :], preferred_element_type=f32)
 
     def attend_cached(g):
@@ -418,6 +419,9 @@
                 send(nsend.at[i], nrecv.at[j], s_n.at[i], r_n.at[j], row_peer(0, b))
 
     grad_terms()
+    for d in reversed(order[1:]):
+        owner = (y + d) % n
+        send(kvsend.at[owner], kvpart.at[y], s_kv.at[d], r_kv.at[y], row_peer(0, d))
     attend_cached(0)
     grad_send()
     attend_cached(1)
@@ -432,8 +436,10 @@
     fresh = fresh.astype(bf16)
     keys[cached:, :] = norm_rows(fresh[:, :head], kgain)
     vals[cached:, 0:head] = fresh[:, head:]
-    for g in (3, 2, 1, 0):
-        attend_new(g)
+    attend_new(3)
+    attend_new(2)
+    attend_new(1)
+    attend_new(0)
 
     for j in range(1, n):
         arrived(nrecv.at[j], s_n.at[j], r_n.at[j])

time: 100 us -> 101 us (1.010)
  no operation moved by 1% of the time
where the time goes in v4:
time: 101 us
  Pallas kernels  97.9 us (97%)
  local copies, waits for them, and re-layouts  2.05 us (2%)
    pallas_call x1, Pallas kernels, body(): pl.pallas_call(functools.partial(kernel, n), name='attention_block', out_...  97.9 us
    unnamed x4, local copies, waits for them, and re-layouts  2.05 us

profile of v4, /device:TPU:1, one launch (start us, length us, event | category | flops | bytes accessed | tf_op | source)
XLA Modules:
  0.0 100.6 jit_solution(7993210970946419959)
XLA Ops:
  0.6 97.9 %attention_block.1 = (bf16[192,128]{1,0:T(8,128)(2,1)}, bf16[128,128]{1,0:T(8,128)(2,1)}) custom-call(bf16[192,128]{1,0:T(8,128)(2,1)} %bitcast.8, bf16[384,128]{1,0:T(8,128)(2,1)} %w_query.1, bf16[384,128]{1,0:T(8,128)(2,1)} %w_key.1, bf16[384,128]{1,0:T(8,128)(2,1)} %w_value.1, bf16[192,256]{1,0:T(8,128)(2,1)} %bitcast.7, bf16[2048,128]{1,0:T(8,128)(2,1)} %key_cache.1, ...), custom_call_target="tpu_custom_call" | custom-call | tf_op jit(solution)/shard_map/attention_block/pallas_call | solution.py:542
  98.5 0.0 copy-start
  98.5 1.4 %copy.15 = bf16[128,192]{0,1:T(8,128)(2,1)} copy(bf16[128,192]{0,1:T(8,128)(2,1)} %bitcast.10) | data formatting | bytes 98304
  99.9 0.0 copy-done
  100.0 0.6 copy.16
Async XLA Ops:
  98.5 1.4 %copy-start = (bf16[128,128]{1,0:T(8,128)(2,1)S(1)}, bf16[128,128]{1,0:T(8,128)(2,1)}, u32[]{:S(2)}) copy-start(bf16[128,128]{1,0:T(8,128)(2,1)} %get-tuple-element.9) | copy-start | bytes 98308
